TPU v7x, 32 devices: a whole 2x2x4 slice. The times are simulated.
32 devices in a mesh: dp: 2 (over x), row: 2 (over core), col: 8 (over z, y).
Axes of the slice: x: 2, y: 2, z: 4, core: 2. Of those that a mesh axis runs over, the one named last changes fastest.
Arguments:
- tokens: bfloat16 [12288, 1024], P(('dp', 'col'), 'row'), may hold values from -6 to 6
- segments: int32 [12, 1024], P(('dp', 'row')), may hold values from 0 to 17, as said below
- attend_gain: bfloat16 [1024], P('row'), may hold values from 0.5 to 1.5
- attend_shift: bfloat16 [1024], P('row'), may hold values from -1.75 to 1.75
- input_weight: bfloat16 [1024, 3, 1024], P('row', None, 'col'), may hold values from -0.1875 to 0.1875
- input_bias: bfloat16 [2, 1024], P(None, 'col'), may hold values from -3 to 3
- output_weight: bfloat16 [1024, 1024], P('col', 'row'), may hold values from -1.5 to 1.5
- output_bias: bfloat16 [1024], P('row'), may hold values from -1.75 to 1.75
- feed_gain: bfloat16 [1024], P('row'), may hold values from 0.5 to 1.5
- feed_shift: bfloat16 [1024], P('row'), may hold values from -1.75 to 1.75
- up_weight: bfloat16 [1024, 4096], P('row', 'col'), may hold values from -0.1875 to 0.1875
- up_bias: bfloat16 [4096], P('col'), may hold values from -1.75 to 1.75
- down_weight: bfloat16 [4096, 1024], P('col', 'row'), may hold values from -0.09375 to 0.09375
- down_bias: bfloat16 [1024], P('row'), may hold values from -1.75 to 1.75
- grad_out: bfloat16 [12288, 1024], P(('dp', 'col'), 'row'), may hold values from -6 to 6
Outputs:
- layer_out: bfloat16 [12288, 1024], P(('dp', 'col'), 'row')
- grad_tokens: float32 [12288, 1024], P(('dp', 'col'), 'row')
- grad_attend_gain: float32 [1024], P('row')
- grad_attend_shift: float32 [1024], P('row')
- grad_input_weight: float32 [1024, 3, 1024], P('row', None, 'col')
- grad_input_bias: float32 [2, 1024], P(None, 'col')
- grad_output_weight: float32 [1024, 1024], P('col', 'row')
- grad_output_bias: float32 [1024], P('row')
- grad_feed_gain: float32 [1024], P('row')
- grad_feed_shift: float32 [1024], P('row')
- grad_up_weight: float32 [1024, 4096], P('row', 'col')
- grad_up_bias: float32 [4096], P('col')
- grad_down_weight: float32 [4096, 1024], P('col', 'row')
- grad_down_bias: float32 [1024], P('row')
Inputs may be any that keep to these rules, and one draw needn't show every extreme that they name: `segments`: along each sequence the numbers never fall; documents are numbered 1, 2, 3 in order; every sequence ends in padding marked 0, and 0 appears nowhere else. The first sequence reaches the largest document number.
All inputs are finite; a program needn't handle non-finite values.
Results may differ from a plain program's by a relative error of at most 0.0092.
Values may be sent and summed in bfloat16 or wider, within the bound.
No kernel may reach another device: no remote copies, remote signals or barrier semaphores. Data moves between devices by JAX's collectives and lax.ppermute only.
A program may use at most 192 MiB of HBM per device.

v0:
```python
from functools import partial
import jax
import jax.numpy as jnp
from jax import lax
from jax.sharding import PartitionSpec as P

HD = 64
epsilon = 1e-05
masked_score = -1000000000.0


def for_sending(shard):

    def short(part):
        return part.astype(jnp.bfloat16) if part.dtype == jnp.float32 else part

    return jax.tree.map(short, shard)


def product(left_side, right_side, flipped):
    if flipped:
        return lax.dot_general(
            left_side, right_side, (((1,), (1,)), ((), ())), preferred_element_type=jnp.float32
        )
    return jnp.dot(left_side, right_side, preferred_element_type=jnp.float32)


def inner_rows(left_side, right_side):
    return lax.dot_general(
        left_side, right_side, (((0,), (0,)), ((), ())), preferred_element_type=jnp.float32
    )


def width_totals(first_sum, second_sum):
    return lax.psum((first_sum, second_sum), "row")


def norm_forward(values, gain, shift):
    features = values.shape[1] * lax.axis_size("row")
    totals, square = width_totals(
        jnp.sum(values, axis=1, keepdims=True), jnp.sum(values * values, axis=1, keepdims=True)
    )
    average = totals / features
    inverse = lax.rsqrt(square / features - average * average + epsilon)
    normed = (values - average) * inverse
    return (normed * gain + shift, normed, inverse)


def norm_backward(grad_norm, normed, inverse, gain):
    features = grad_norm.shape[1] * lax.axis_size("row")
    scaled = grad_norm * gain
    totals, against = width_totals(
        jnp.sum(scaled, axis=1, keepdims=True), jnp.sum(scaled * normed, axis=1, keepdims=True)
    )
    returned = inverse * (scaled - totals / features - normed * against / features)
    return (returned, jnp.sum(grad_norm * normed, axis=0), jnp.sum(grad_norm, axis=0))


def col_then_row(shard_in, weight, flipped):
    gathered = lax.all_gather(shard_in, "col", axis=0, tiled=True)
    return (
        gathered,
        lax.psum_scatter(
            product(gathered, weight, flipped), "row", scatter_dimension=0, tiled=True
        ),
    )


def row_then_col(shard_in, weight, flipped):
    gathered = lax.all_gather(for_sending(shard_in), "row", axis=0, tiled=True).astype(
        shard_in.dtype
    )
    row_count = gathered.shape[0] // lax.axis_size("col")
    block_rows = lax.dynamic_slice_in_dim(
        gathered, jnp.int32(0), lax.axis_size("col") * row_count, 0
    )
    return (
        gathered,
        lax.psum_scatter(
            product(block_rows, weight, flipped), "col", scatter_dimension=0, tiled=True
        ),
    )


def head_masks(labels):
    positions = jnp.arange(labels.shape[0])
    causal = positions[None, :] <= positions[:, None]
    matching = (labels[:, None] == labels[None, :]) & (labels[:, None] > 0)
    return causal & (matching | (positions[:, None] == positions[None, :]))


def scores_of(queries, key_rows, labels):
    scaling = queries.shape[-1] ** (-0.5)
    products = (
        jnp.einsum("qhd,khd->hqk", queries, key_rows, preferred_element_type=jnp.float32) * scaling
    )
    return jnp.where(head_masks(labels)[None], products, masked_score)


def attend_forward(packed):
    queries, key_rows, values, labels = packed
    scores = scores_of(queries, key_rows, labels)
    highest = jnp.max(scores, axis=2, keepdims=True)
    weights = jnp.exp(scores - highest)
    totals = jnp.sum(weights, axis=2, keepdims=True)
    chances = (weights / totals).astype(jnp.bfloat16)
    attended = jnp.einsum("hqk,khd->qhd", chances, values, preferred_element_type=jnp.float32)
    return (attended.astype(jnp.bfloat16), highest + jnp.log(totals))


def attend_backward(packed):
    queries, key_rows, values, labels, summary, grad_attended = packed
    scaling = queries.shape[-1] ** (-0.5)
    chances = jnp.exp(scores_of(queries, key_rows, labels) - summary)
    rounded = chances.astype(jnp.bfloat16)
    grad_values = jnp.einsum(
        "hqk,qhd->khd", rounded, grad_attended, preferred_element_type=jnp.float32
    )
    grad_chances = jnp.einsum(
        "qhd,khd->hqk", grad_attended, values, preferred_element_type=jnp.float32
    )
    grad_scores = chances * (grad_chances - jnp.sum(chances * grad_chances, axis=2, keepdims=True))
    grad_scores = grad_scores.astype(jnp.bfloat16)
    grad_queries = (
        jnp.einsum("hqk,khd->qhd", grad_scores, key_rows, preferred_element_type=jnp.float32)
        * scaling
    )
    grad_keys = (
        jnp.einsum("hqk,qhd->khd", grad_scores, queries, preferred_element_type=jnp.float32)
        * scaling
    )
    return (grad_queries, grad_keys, grad_values)


def per_device(
    tokens,
    segments,
    attend_gain,
    attend_shift,
    input_weight,
    input_bias,
    output_weight,
    output_bias,
    feed_gain,
    feed_shift,
    up_weight,
    up_bias,
    down_weight,
    down_bias,
    grad_out,
):
    inputs = tokens.astype(jnp.float32)
    seq_count, length = segments.shape
    head_width = input_weight.shape[2]
    heads_here = head_width // HD
    input_flat = input_weight.reshape(input_weight.shape[0], 3 * head_width)
    gain_one = attend_gain.astype(jnp.float32)
    gain_two = feed_gain.astype(jnp.float32)
    first_out, normed_one, inverse_one = norm_forward(
        inputs, gain_one, attend_shift.astype(jnp.float32)
    )
    first_low = first_out.astype(jnp.bfloat16)
    first_all, projected = col_then_row(first_low, input_flat, False)
    zero_row = jnp.zeros((1, head_width), jnp.float32)
    bias_rows = jnp.concatenate(
        [input_bias[0:1].astype(jnp.float32), zero_row, input_bias[1:2].astype(jnp.float32)], axis=1
    )
    projected = (projected + bias_rows).astype(jnp.bfloat16)
    shaped = projected.reshape(seq_count, length, 3, heads_here, HD)
    queries = shaped[:, :, 0]
    key_rows = shaped[:, :, 1]
    values = shaped[:, :, 2]
    attended, summary = lax.map(attend_forward, (queries, key_rows, values, segments))
    attended_flat = attended.reshape(seq_count * length, head_width)
    attended_all, branch_one = row_then_col(attended_flat, output_weight, False)
    middle = inputs + (branch_one + output_bias.astype(jnp.float32))
    second_out, normed_two, inverse_two = norm_forward(
        middle, gain_two, feed_shift.astype(jnp.float32)
    )
    second_low = second_out.astype(jnp.bfloat16)
    gelu_tanh = partial(jax.nn.gelu, approximate=True)
    second_all, hidden_pre = col_then_row(second_low, up_weight, False)
    hidden_pre = hidden_pre + up_bias.astype(jnp.float32)
    hidden = gelu_tanh(hidden_pre).astype(jnp.bfloat16)
    hidden_all, branch_two = row_then_col(hidden, down_weight, False)
    result = middle + (branch_two + down_bias.astype(jnp.float32))
    layer_out = result.astype(jnp.bfloat16)
    grad_top = grad_out.astype(jnp.float32)
    grad_down_bias = jnp.sum(grad_top, axis=0)
    output_all, grad_hidden = col_then_row(grad_out, down_weight, True)
    gelu_unused, gelu_pull = jax.vjp(gelu_tanh, hidden_pre)
    grad_pre = gelu_pull(grad_hidden)[0].astype(jnp.bfloat16)
    grad_up_bias = jnp.sum(grad_pre.astype(jnp.float32), axis=0)
    grad_down_weight = inner_rows(hidden_all, output_all)
    pre_all, grad_second = row_then_col(grad_pre, up_weight, True)
    grad_up_weight = inner_rows(second_all, pre_all)
    grad_norm_two, grad_feed_gain, grad_feed_shift = norm_backward(
        grad_second, normed_two, inverse_two, gain_two
    )
    grad_middle = grad_top + grad_norm_two
    grad_branch = grad_middle.astype(jnp.bfloat16)
    grad_output_bias = jnp.sum(grad_branch.astype(jnp.float32), axis=0)
    branch_all, grad_attended = col_then_row(grad_branch, output_weight, True)
    grad_output_weight = inner_rows(attended_all, branch_all)
    grad_heads = grad_attended.astype(jnp.bfloat16).reshape(seq_count, length, heads_here, HD)
    grad_queries, grad_keys, grad_values = lax.map(
        attend_backward, (queries, key_rows, values, segments, summary, grad_heads)
    )
    grad_projected = jnp.stack([grad_queries, grad_keys, grad_values], axis=2).astype(jnp.bfloat16)
    grad_projected = grad_projected.reshape(seq_count * length, 3 * head_width)
    slot_sums = jnp.sum(grad_projected.astype(jnp.float32), axis=0).reshape(3, head_width)
    grad_input_bias = jnp.stack([slot_sums[0], slot_sums[2]])
    projected_all, grad_first = row_then_col(grad_projected, input_flat, True)
    grad_input_weight = inner_rows(first_all, projected_all).reshape(input_weight.shape)
    grad_norm_one, grad_attend_gain, grad_attend_shift = norm_backward(
        grad_first, normed_one, inverse_one, gain_one
    )
    grad_tokens = grad_middle + grad_norm_one
    grad_input_weight, grad_output_weight, grad_up_weight, grad_down_weight = lax.psum(
        (grad_input_weight, grad_output_weight, grad_up_weight, grad_down_weight), "dp"
    )
    (
        grad_attend_gain,
        grad_attend_shift,
        grad_output_bias,
        grad_feed_gain,
        grad_feed_shift,
        grad_down_bias,
    ) = lax.psum(
        (
            grad_attend_gain,
            grad_attend_shift,
            grad_output_bias,
            grad_feed_gain,
            grad_feed_shift,
            grad_down_bias,
        ),
        ("dp", "col"),
    )
    grad_input_bias, grad_up_bias = lax.psum((grad_input_bias, grad_up_bias), ("dp", "row"))
    return (
        layer_out,
        grad_tokens,
        grad_attend_gain,
        grad_attend_shift,
        grad_input_weight,
        grad_input_bias,
        grad_output_weight,
        grad_output_bias,
        grad_feed_gain,
        grad_feed_shift,
        grad_up_weight,
        grad_up_bias,
        grad_down_weight,
        grad_down_bias,
    )


def solution(mesh):
    in_specs = (
        P(("dp", "col"), "row"),
        P(("dp", "row"), None),
        P("row"),
        P("row"),
        P("row", None, "col"),
        P(None, "col"),
        P("col", "row"),
        P("row"),
        P("row"),
        P("row"),
        P("row", "col"),
        P("col"),
        P("col", "row"),
        P("row"),
        P(("dp", "col"), "row"),
    )
    out_specs = (
        P(("dp", "col"), "row"),
        P(("dp", "col"), "row"),
        P("row"),
        P("row"),
        P("row", None, "col"),
        P(None, "col"),
        P("col", "row"),
        P("row"),
        P("row"),
        P("row"),
        P("row", "col"),
        P("col"),
        P("col", "row"),
        P("row"),
    )
    return jax.shard_map(
        per_device, mesh=mesh, in_specs=in_specs, out_specs=out_specs, check_vma=False
    )
```

profile of v0, /device:TPU:0, one launch (start us, length us, event | category | flops | bytes accessed | tf_op | source)
XLA Modules:
  0.0 1655.1 jit_solution(5159023049874539472)
XLA Ops:
  17.0 100.2 %all-gather.9.cloned.1.call-done = bf16[6144,512]{1,0:T(8,128)(2,1)} async-done(((bf16[768,512]{1,0:T(8,128)(2,1)}), bf16[6144,512]{1,0:T(8,128)(2,1)}) %all-gather.9.cloned.1.call-update) | async-done | bytes 6291472 | tf_op jit(solution)/shard_map/all_gather | solution.py:60
  117.2 9.9 fusion.84
  127.8 14.9 reduce-scatter.9.cloned.1.call-done
  148.0 7.4 reshape.240
  159.4 30.3 %while.26 = (s32[]{:T(128)}, bf16[3,1024,2,64]{1,3,2,0:T(8,128)(2,1)}, f32[3,2,1024,1]{2,1,3,0:T(2,128)}, bf16[3,1024,2,64]{1,3,2,0:T(8,128)(2,1)S(1)}, s32[3,10...) while((s32[]{:T(128)}, ...), condition=%wide.region_8.9_spmd, body=%wide.region_5.8_spmd.sunk | while | flops 568458240 | bytes 30494820 | solution.py:173
  193.4 11.2 all-gather.11.cloned.1.call-done
  204.6 7.7 fusion.85
  215.2 206.0 %reduce-scatter.11.cloned.1.call-done = f32[768,512]{1,0:T(8,128)} async-done(((f32[6144,512]{1,0:T(8,128)}), f32[768,512]{1,0:T(8,128)}) %reduce-scatter.11.cloned.1.call-update) | async-done | bytes 1572880 | tf_op jit(solution)/shard_map/reduce_scatter | solution.py:79
  427.5 93.5 %all-gather.17.cloned.1.call-done = bf16[6144,512]{1,0:T(8,128)(2,1)} async-done(((bf16[768,512]{1,0:T(8,128)(2,1)}), bf16[6144,512]{1,0:T(8,128)(2,1)}) %all-gather.17.cloned.1.call-update) | async-done | bytes 6291472 | tf_op jit(solution)/shard_map/all_gather | solution.py:60
  521.0 9.5 fusion.88
  530.6 89.9 %all-gather.13.cloned.1.call-done = bf16[6144,512]{1,0:T(8,128)(2,1)} async-done(((bf16[768,512]{1,0:T(8,128)(2,1)}), bf16[6144,512]{1,0:T(8,128)(2,1)}) %all-gather.13.cloned.1.call-update) | async-done | bytes 6291472 | tf_op jit(solution)/shard_map/all_gather | solution.py:60
  620.6 10.6 fusion.86
  631.9 9.9 reduce-scatter.17.cloned.1.call-done
  641.8 25.7 %reduce-scatter.13.cloned.1.call-done = f32[3072,512]{1,0:T(8,128)} async-done(((f32[6144,512]{1,0:T(8,128)}), f32[3072,512]{1,0:T(8,128)}) %reduce-scatter.13.cloned.1.call-update) | async-done | bytes 6291472 | tf_op jit(solution)/shard_map/reduce_scatter | solution.py:63
  667.5 10.0 convert_reduce_fusion
  678.2 18.7 %all-gather.19.cloned.1.call-done = bf16[6144,512]{1,0:T(8,128)(2,1)} async-done(((bf16[3072,512]{1,0:T(8,128)(2,1)}), bf16[6144,512]{1,0:T(8,128)(2,1)}) %all-gather.19.cloned.1.call-update) | async-done | bytes 6291472 | tf_op jit(solution)/shard_map/all_gather | solution.py:70
  696.8 9.5 fusion.89
  706.4 9.8 all-gather.15.cloned.1.call-done
  716.2 9.2 fusion.87
  726.1 202.3 %reduce-scatter.19.cloned.1.call-done = f32[768,512]{1,0:T(8,128)} async-done(((f32[6144,512]{1,0:T(8,128)}), f32[768,512]{1,0:T(8,128)}) %reduce-scatter.19.cloned.1.call-update) | async-done | bytes 1572880 | tf_op jit(solution)/shard_map/reduce_scatter | solution.py:79
  933.8 204.6 %reduce-scatter.15.cloned.1.call-done = f32[768,512]{1,0:T(8,128)} async-done(((f32[6144,512]{1,0:T(8,128)}), f32[768,512]{1,0:T(8,128)}) %reduce-scatter.15.cloned.1.call-update) | async-done | bytes 1572880 | tf_op jit(solution)/shard_map/reduce_scatter | solution.py:79
  1142.0 97.9 %all-gather.21.cloned.1.call-done = bf16[6144,512]{1,0:T(8,128)(2,1)} async-done(((bf16[768,512]{1,0:T(8,128)(2,1)}), bf16[6144,512]{1,0:T(8,128)(2,1)}) %all-gather.21.cloned.1.call-update) | async-done | bytes 6291472 | tf_op jit(solution)/shard_map/all_gather | solution.py:60
  1239.9 6.2 fusion.90
  1246.3 9.4 reduce-scatter.21.cloned.1.call-done
  1262.3 50.3 %while.27 = (s32[]{:T(128)}, bf16[3,1024,2,64]{1,3,2,0:T(8,128)(2,1)}, bf16[3,1024,2,64]{1,3,2,0:T(8,128)(2,1)}, bf16[3,1024,2,64]{1,3,2,0:T(8,128)(2,1)}, bf16[...) while((s32[]{:T(128)}, ...), condition=%wide.region_25.26_spmd, body=%wide.region_23.25_spmd.sunk | while | flops 1380187136 | bytes 89472296 | solution.py:206
  1319.4 15.9 all-gather.23.cloned.1.call-done
  1335.2 8.9 fusion.91
  1344.2 9.2 fusion.93
  1353.4 9.2 fusion.94
  1370.5 8.2 all-reduce.1
  1378.8 174.1 %reduce-scatter.23.cloned.1.call-done = f32[768,512]{1,0:T(8,128)} async-done(((f32[6144,512]{1,0:T(8,128)}), f32[768,512]{1,0:T(8,128)}) %reduce-scatter.23.cloned.1.call-update) | async-done | bytes 1572880 | tf_op jit(solution)/shard_map/reduce_scatter | solution.py:79
  1555.1 76.0 %all-reduce = (f32[512]{0:T(512)}, f32[512]{0:T(512)}, f32[512]{0:T(512)}, f32[512]{0:T(512)}, f32[512]{0:T(512)}, /*index=5*/f32[512]{0:T(512)}) all-reduce(f32[512]{0:T(512)S(1)} %get-tuple-element.140, f32[512]{0:T(512)S(1)} %get-tuple-element.145, ...), channel_id=1, replica_groups=mesh['dp'=2,'row'=2,'col'=8] {'dp','col'}, use_global_device_ids=true, to_apply=%region_32.33 | all-reduce | flops 3072 | bytes 24576 | tf_op jit(solution)/shard_map/psum | solution.py:229
  (277 shorter events, 164.1 us)
Async XLA Ops:
  7.2 613.4 %copy-start = (bf16[512,512]{1,0:T(8,128)(2,1)S(1)}, bf16[512,512]{1,0:T(8,128)(2,1)}, u32[]{:S(2)}) copy-start(bf16[512,512]{1,0:T(8,128)(2,1)} %param.29) | copy-start | bytes 1572868
  7.2 110.0 %all-gather.9.cloned.1.call-start = ((), (), s32[]{:S(2)}) async-start(), calls=%async_computation.8 | async-start | bytes 7077888 | tf_op jit(solution)/shard_map/all_gather | solution.py:60
  15.8 126.9 %reduce-scatter.9.cloned.1.call-start = ((), (), s32[]{:S(2)}) async-start(), calls=%async_computation.9 | async-start | bytes 14155776 | tf_op jit(solution)/shard_map/reduce_scatter | solution.py:63
  17.0 110.1 %copy-start.11 = (bf16[512,3,128]{0,2,1:T(8,128)(2,1)}, bf16[512,3,128]{0,2,1:T(8,128)(2,1)S(1)}, u32[]{:S(2)}) copy-start(bf16[512,3,128]{0,2,1:T(8,128)(2,1)S(1)} %copy.42) | copy-start | bytes 1179652
  127.1 77.4 %all-gather.11.cloned.1.call-start = ((), (), s32[]{:S(2)}) async-start(), calls=%async_computation.10 | async-start | bytes 2359296 | tf_op jit(solution)/shard_map/all_gather | solution.py:70
  193.3 227.9 %reduce-scatter.11.cloned.1.call-start = ((), (), s32[]{:S(2)}) async-start(), calls=%async_computation.11 | async-start | bytes 14155776 | tf_op jit(solution)/shard_map/reduce_scatter | solution.py:79
  212.4 208.8 %copy-start.2 = (bf16[768,512]{1,0:T(8,128)(2,1)S(1)}, bf16[768,512]{1,0:T(8,128)(2,1)}, u32[]{:S(2)}) copy-start(bf16[768,512]{1,0:T(8,128)(2,1)} %param.19) | copy-start | bytes 2359300
  212.4 308.7 %copy-start.14 = (bf16[512,512]{1,0:T(8,128)(2,1)S(1)}, bf16[512,512]{1,0:T(8,128)(2,1)}, u32[]{:S(2)}) copy-start(bf16[512,512]{1,0:T(8,128)(2,1)} %param.31) | copy-start | bytes 1572868
  212.4 308.6 %all-gather.17.cloned.1.call-start = ((), (), s32[]{:S(2)}) async-start(), calls=%async_computation.16 | async-start | bytes 7077888 | tf_op jit(solution)/shard_map/all_gather | solution.py:60
  213.0 407.6 %all-gather.13.cloned.1.call-start = ((), (), s32[]{:S(2)}) async-start(), calls=%async_computation.12 | async-start | bytes 7077888 | tf_op jit(solution)/shard_map/all_gather | solution.py:60
  427.4 214.4 %reduce-scatter.17.cloned.1.call-start = ((), (), s32[]{:S(2)}) async-start(), calls=%async_computation.17 | async-start | bytes 18874368 | tf_op jit(solution)/shard_map/reduce_scatter | solution.py:63
  530.6 136.9 %reduce-scatter.13.cloned.1.call-start = ((), (), s32[]{:S(2)}) async-start(), calls=%async_computation.13 | async-start | bytes 18874368 | tf_op jit(solution)/shard_map/reduce_scatter | solution.py:63
  631.2 65.6 %all-gather.19.cloned.1.call-start = ((), (), s32[]{:S(2)}) async-start(), calls=%async_computation.18 | async-start | bytes 9437184 | tf_op jit(solution)/shard_map/all_gather | solution.py:70
  677.5 38.6 %all-gather.15.cloned.1.call-start = ((), (), s32[]{:S(2)}) async-start(), calls=%async_computation.14 | async-start | bytes 9437184 | tf_op jit(solution)/shard_map/all_gather | solution.py:70
  678.1 250.3 %reduce-scatter.19.cloned.1.call-start = ((), (), s32[]{:S(2)}) async-start(), calls=%async_computation.19 | async-start | bytes 14155776 | tf_op jit(solution)/shard_map/reduce_scatter | solution.py:79
  706.3 432.1 %reduce-scatter.15.cloned.1.call-start = ((), (), s32[]{:S(2)}) async-start(), calls=%async_computation.15 | async-start | bytes 14155776 | tf_op jit(solution)/shard_map/reduce_scatter | solution.py:79
  725.4 203.0 %copy-start.25 = (f32[768]{0:T(1024)S(1)}, f32[768]{0:T(1024)}, u32[]{:S(2)}) copy-start(f32[768]{0:T(1024)} %copy-done.24) | copy-start | bytes 9220
  725.4 203.0 %copy-start.27 = (f32[768]{0:T(1024)S(1)}, f32[768]{0:T(1024)}, u32[]{:S(2)}) copy-start(f32[768]{0:T(1024)} %copy-done.26) | copy-start | bytes 9220
  725.4 203.0 %copy-start.34 = (f32[512]{0:T(512)S(1)}, f32[512]{0:T(512)}, u32[]{:S(2)}) copy-start(f32[512]{0:T(512)} %convert_element_type.98) | copy-start | bytes 6148
  725.4 413.0 %copy-start.13 = (bf16[768,512]{1,0:T(8,128)(2,1)S(1)}, bf16[768,512]{1,0:T(8,128)(2,1)}, u32[]{:S(2)}) copy-start(bf16[768,512]{1,0:T(8,128)(2,1)} %param.33) | copy-start | bytes 2359300
  725.4 514.5 %all-gather.21.cloned.1.call-start = ((), (), s32[]{:S(2)}) async-start(), calls=%async_computation.20 | async-start | bytes 7077888 | tf_op jit(solution)/shard_map/all_gather | solution.py:60
  1142.0 113.7 %reduce-scatter.21.cloned.1.call-start = ((), (), s32[]{:S(2)}) async-start(), calls=%async_computation.21 | async-start | bytes 4718592 | tf_op jit(solution)/shard_map/reduce_scatter | solution.py:63
  1246.2 89.0 %all-gather.23.cloned.1.call-start = ((), (), s32[]{:S(2)}) async-start(), calls=%async_computation.22 | async-start | bytes 7077888 | tf_op jit(solution)/shard_map/all_gather | solution.py:70
  1319.3 233.5 %reduce-scatter.23.cloned.1.call-start = ((), (), s32[]{:S(2)}) async-start(), calls=%async_computation.23 | async-start | bytes 14155776 | tf_op jit(solution)/shard_map/reduce_scatter | solution.py:79
  1344.1 297.2 %all-reduce.9.cloned.1.call-start = ((), (), s32[]{:S(2)}) async-start(), calls=%async_computation.24 | async-start | bytes 6291456 | tf_op jit(solution)/shard_map/psum | solution.py:219
  1367.8 185.0 %copy-start.3 = (bf16[768,512]{1,0:T(8,128)(2,1)S(1)}, bf16[768,512]{1,0:T(8,128)(2,1)}, u32[]{:S(2)}) copy-start(bf16[768,512]{1,0:T(8,128)(2,1)} %param.19) | copy-start | bytes 2359300
  1367.8 185.0 %copy-start.29 = (f32[768]{0:T(1024)S(1)}, f32[768]{0:T(1024)}, u32[]{:S(2)}) copy-start(f32[768]{0:T(1024)} %copy-done.28) | copy-start | bytes 9220
  1367.8 185.0 %copy-start.31 = (f32[768]{0:T(1024)S(1)}, f32[768]{0:T(1024)}, u32[]{:S(2)}) copy-start(f32[768]{0:T(1024)} %copy-done.30) | copy-start | bytes 9220
  1367.8 185.0 %copy-start.33 = (f32[512]{0:T(512)S(1)}, f32[512]{0:T(512)}, u32[]{:S(2)}) copy-start(f32[512]{0:T(512)} %copy-done.32) | copy-start | bytes 6148
  1367.8 187.2 %copy-start.36 = (f32[512]{0:T(512)S(1)}, f32[512]{0:T(512)}, u32[]{:S(2)}) copy-start(f32[512]{0:T(512)} %get-tuple-element.138) | copy-start | bytes 6148
  1367.8 187.2 %copy-start.37 = (f32[512]{0:T(512)S(1)}, f32[512]{0:T(512)}, u32[]{:S(2)}) copy-start(f32[512]{0:T(512)} %get-tuple-element.144) | copy-start | bytes 6148
  1367.9 265.8 %copy-start.9 = (f32[768,512]{1,0:T(8,128)S(1)}, f32[768,512]{1,0:T(8,128)}, u32[]{:S(2)}) copy-start(f32[768,512]{1,0:T(8,128)} %get-tuple-element.214) | copy-start | bytes 4718596
  (47 other events, 550.7 us)
Sparse Core Ops, SparseCore 0:
  15.9 101.2 all-gather.8
  127.2 15.3 reduce-scatter.8
  193.4 11.0 all-gather.10
  212.5 208.6 reduce-scatter.10
  423.2 97.7 all-gather.16
  523.7 96.8 all-gather.12
  622.9 18.9 reduce-scatter.16
  644.1 23.3 reduce-scatter.12
  677.6 19.1 all-gather.18
  698.2 17.9 all-gather.14
  719.8 208.5 reduce-scatter.18
  931.8 206.5 reduce-scatter.14
  1142.1 97.7 all-gather.20
  1246.3 9.3 reduce-scatter.20
  1319.4 15.7 all-gather.22
  1344.2 208.5 reduce-scatter.22
  1556.3 84.9 all-reduce.8
where the time goes:
time: 1660 us
  waiting for transfers between devices  1290 us (78%)
  matrix products  142 us (9%)
  blocking collectives  94.5 us (6%)
  other arithmetic  67 us (4%)
  local copies, waits for them, and re-layouts  45.4 us (3%)
    reduce_scatter x4, waiting for transfers between devices, row_then_col(): lax.psum_scatter(product(block_rows, weight, flipped), 'col', scatter_dim...  787 us
    all_gather x4, waiting for transfers between devices, col_then_row(): gathered = lax.all_gather(shard_in, 'col', axis=0, tiled=True)  382 us
    psum x1, blocking collectives, per_device(): lax.psum((grad_attend_gain, grad_attend_shift, grad_output_bias, grad_fee...  76 us
    reduce_scatter x4, waiting for transfers between devices, col_then_row(): lax.psum_scatter(product(gathered, weight, flipped), 'row', scatter_dimen...  59.9 us
    all_gather x4, waiting for transfers between devices, row_then_col(): lax.all_gather(for_sending(shard_in), 'row', axis=0, tiled=True)  55.5 us
    dot_general x4, matrix products, product(): return jnp.dot(left_side, right_side, preferred_element_type=jnp.float32)  37.4 us
    dot_general x4, matrix products, product(): lax.dot_general(left_side, right_side, (((1,), (1,)), ((), ())), preferre...  34.1 us
  transfers between devices with their start and end apart: 17, of which 17 were waited for; matrix products, arithmetic and copies ran while one was open for 5% of the time, Pallas kernels for 0%

commit v1 on v0

--- a/solution.py
+++ b/solution.py
@@ -57,7 +57,16 @@
 
 
 def col_then_row(shard_in, weight, flipped):
-    gathered = lax.all_gather(shard_in, "col", axis=0, tiled=True)
+    ways = lax.axis_size("col")
+    up = [(d, (d + 1) % ways) for d in range(ways)]
+    down = [(d, (d - 1) % ways) for d in range(ways)]
+    earlier, later = ([shard_in], [shard_in])
+    for _ in range(ways // 2):
+        earlier.append(lax.ppermute(earlier[-1], "col", up))
+    for _ in range((ways - 1) // 2):
+        later.append(lax.ppermute(later[-1], "col", down))
+    line = jnp.concatenate([*earlier[::-1], *later[1:]], axis=0)
+    gathered = jnp.roll(line, (lax.axis_index("col") - ways // 2) * shard_in.shape[0], axis=0)
     return (
         gathered,
         lax.psum_scatter(

time: 1660 us -> 1750 us (1.054)
  starting transfers between devices: 1.28 us -> 104 us
  waiting for transfers between devices: 1290 us -> 1220 us
  local copies, waits for them, and re-layouts: 45.4 us -> 74.3 us
    ppermute x0 -> x28, waiting for transfers between devices: none -> 456 us  [the longest x16 428 us: col_then_row(): earlier.append(lax.ppermute(earlier[-1], 'col', up))]
    all_gather x4 -> x0, waiting for transfers between devices: 382 us -> none  [col_then_row(): gathered = lax.all_gather(shard_in, 'col', axis=0, tiled=True)]
    reduce_scatter x4, waiting for transfers between devices: 787 us -> 663 us  [row_then_col(): lax.psum_scatter(product(block_rows, weight, flipped), 'col', scatter_dim...]
    ppermute x0 -> x28, starting transfers between devices: none -> 102 us  [the longest x12 76.8 us: col_then_row(): later.append(lax.ppermute(later[-1], 'col', down))]
    unnamed x95 -> x125, local copies, waits for them, and re-layouts: 14.4 us -> 41 us
  transfers between devices with their start and end apart: 17 -> 41, of which waited for: 17 -> 32; matrix products, arithmetic and copies ran while one was open for 5% -> 6% of each run, Pallas kernels for 0% -> 0%
where the time goes in v1:
time: 1750 us; the launch traced here: 1740 us
  waiting for transfers between devices  1220 us (70%)
  matrix products  156 us (9%)
  starting transfers between devices  104 us (6%)
  blocking collectives  94.5 us (5%)
  local copies, waits for them, and re-layouts  74.3 us (4%)
  other arithmetic  73.4 us (4%)
    reduce_scatter x4, waiting for transfers between devices, row_then_col(): lax.psum_scatter(product(block_rows, weight, flipped), 'col', scatter_dim...  663 us
    ppermute x16, waiting for transfers between devices, col_then_row(): earlier.append(lax.ppermute(earlier[-1], 'col', up))  428 us
    ppermute x12, starting transfers between devices, col_then_row(): later.append(lax.ppermute(later[-1], 'col', down))  76.8 us
    psum x1, blocking collectives, per_device(): lax.psum((grad_attend_gain, grad_attend_shift, grad_output_bias, grad_fee...  76 us
    all_gather x4, waiting for transfers between devices, row_then_col(): lax.all_gather(for_sending(shard_in), 'row', axis=0, tiled=True)  55.7 us
    reduce_scatter x4, waiting for transfers between devices, col_then_row(): lax.psum_scatter(product(gathered, weight, flipped), 'row', scatter_dimen...  43.3 us
    unnamed x125, local copies, waits for them, and re-layouts  41 us
    dot_general x4, matrix products, product(): return jnp.dot(left_side, right_side, preferred_element_type=jnp.float32)  40.2 us
  transfers between devices with their start and end apart: 41, of which 32 were waited for; matrix products, arithmetic and copies ran while one was open for 6% of the time, Pallas kernels for 0%

profile of v1, /device:TPU:0, one launch (start us, length us, event | category | flops | bytes accessed | tf_op | source)
XLA Modules:
  0.0 1740.5 jit_solution(3083657808223645787)
XLA Ops:
  17.2 20.9 %collective-permute-done = bf16[768,512]{1,0:T(8,128)(2,1)S(1)} collective-permute-done((bf16[768,512]{1,0:T(8,128)(2,1)S(1)}, bf16[768,512]{1,0:T(8,128)(2,1)S(1)}, u32[]{:S(2)}, u32[]{:S(2)}) %collective-permute-start) | collective-permute-done | bytes 786464 | tf_op jit(solution)/shard_map/ppermute | solution.py:65
  42.9 29.0 %collective-permute-done.1 = bf16[768,512]{1,0:T(8,128)(2,1)S(1)} collective-permute-done((bf16[768,512]{1,0:T(8,128)(2,1)S(1)}, bf16[768,512]{1,0:T(8,128)(2,1)S(1)}, u32[]{:S(2)}, u32[]{:S(2)}) %collective-permute-start.1) | collective-permute-done | bytes 786464 | tf_op jit(solution)/shard_map/ppermute | solution.py:65
  77.5 30.6 %collective-permute-done.2 = bf16[768,512]{1,0:T(8,128)(2,1)} collective-permute-done((bf16[768,512]{1,0:T(8,128)(2,1)S(1)}, bf16[768,512]{1,0:T(8,128)(2,1)}, u32[]{:S(2)}, u32[]{:S(2)}) %collective-permute-start.2) | collective-permute-done | bytes 786464 | tf_op jit(solution)/shard_map/ppermute | solution.py:65
  114.0 29.6 %collective-permute-done.3 = bf16[768,512]{1,0:T(8,128)(2,1)} collective-permute-done((bf16[768,512]{1,0:T(8,128)(2,1)}, bf16[768,512]{1,0:T(8,128)(2,1)}, u32[]{:S(2)}, u32[]{:S(2)}) %collective-permute-start.3) | collective-permute-done | bytes 786464 | tf_op jit(solution)/shard_map/ppermute | solution.py:65
  164.8 15.6 reduce-scatter.9.cloned.1.call-done
  201.0 31.3 %while.26 = (s32[]{:T(128)}, bf16[3,1024,2,64]{1,3,2,0:T(8,128)(2,1)}, f32[3,2,1024,1]{2,1,3,0:T(2,128)S(1)}, bf16[3,1024,2,64]{1,3,2,0:T(8,128)(2,1)}, s32[3,10...) while((s32[]{:T(128)}, ...), condition=%wide.region_8.10_spmd, body=%wide.region_5.9_spmd.sunk | while | flops 568458240 | bytes 30494820 | solution.py:182
  257.9 31.8 %collective-permute-done.14 = bf16[768,512]{1,0:T(8,128)(2,1)S(1)} collective-permute-done((bf16[768,512]{1,0:T(8,128)(2,1)S(1)}, bf16[768,512]{1,0:T(8,128)(2,1)S(1)}, u32[]{:S(2)}, u32[]{:S(2)}) %collective-permute-start.14) | collective-permute-done | bytes 786464 | tf_op jit(solution)/shard_map/ppermute | solution.py:65
  294.4 34.4 %collective-permute-done.15 = bf16[768,512]{1,0:T(8,128)(2,1)S(1)} collective-permute-done((bf16[768,512]{1,0:T(8,128)(2,1)S(1)}, bf16[768,512]{1,0:T(8,128)(2,1)S(1)}, u32[]{:S(2)}, u32[]{:S(2)}) %collective-permute-start.15) | collective-permute-done | bytes 786464 | tf_op jit(solution)/shard_map/ppermute | solution.py:65
  329.2 15.0 collective-permute-start.19
  344.2 34.7 %collective-permute-done.16 = bf16[768,512]{1,0:T(8,128)(2,1)S(1)} collective-permute-done((bf16[768,512]{1,0:T(8,128)(2,1)S(1)}, bf16[768,512]{1,0:T(8,128)(2,1)S(1)}, u32[]{:S(2)}, u32[]{:S(2)}) %collective-permute-start.16) | collective-permute-done | bytes 786464 | tf_op jit(solution)/shard_map/ppermute | solution.py:65
  381.4 14.6 collective-permute-done.19
  396.5 24.6 %collective-permute-done.17 = bf16[768,512]{1,0:T(8,128)(2,1)S(1)} collective-permute-done((bf16[768,512]{1,0:T(8,128)(2,1)S(1)}, bf16[768,512]{1,0:T(8,128)(2,1)S(1)}, u32[]{:S(2)}, u32[]{:S(2)}) %collective-permute-start.17) | collective-permute-done | bytes 786464 | tf_op jit(solution)/shard_map/ppermute | solution.py:65
  448.3 90.4 %reduce-scatter.11.cloned.1.call-done = f32[768,512]{1,0:T(8,128)} async-done(((f32[6144,512]{1,0:T(8,128)}), f32[768,512]{1,0:T(8,128)}) %reduce-scatter.11.cloned.1.call-update) | async-done | bytes 1572880 | tf_op jit(solution)/shard_map/reduce_scatter | solution.py:88
  544.9 20.8 %collective-permute-done.7 = bf16[768,512]{1,0:T(8,128)(2,1)S(1)} collective-permute-done((bf16[768,512]{1,0:T(8,128)(2,1)S(1)}, bf16[768,512]{1,0:T(8,128)(2,1)S(1)}, u32[]{:S(2)}, u32[]{:S(2)}) %collective-permute-start.7) | collective-permute-done | bytes 786464 | tf_op jit(solution)/shard_map/ppermute | solution.py:65
  570.4 28.7 %collective-permute-done.8 = bf16[768,512]{1,0:T(8,128)(2,1)S(1)} collective-permute-done((bf16[768,512]{1,0:T(8,128)(2,1)S(1)}, bf16[768,512]{1,0:T(8,128)(2,1)S(1)}, u32[]{:S(2)}, u32[]{:S(2)}) %collective-permute-start.8) | collective-permute-done | bytes 786464 | tf_op jit(solution)/shard_map/ppermute | solution.py:65
  603.8 31.0 %collective-permute-done.9 = bf16[768,512]{1,0:T(8,128)(2,1)S(1)} collective-permute-done((bf16[768,512]{1,0:T(8,128)(2,1)S(1)}, bf16[768,512]{1,0:T(8,128)(2,1)S(1)}, u32[]{:S(2)}, u32[]{:S(2)}) %collective-permute-start.9) | collective-permute-done | bytes 786464 | tf_op jit(solution)/shard_map/ppermute | solution.py:65
  639.7 30.5 %collective-permute-done.10 = bf16[768,512]{1,0:T(8,128)(2,1)S(1)} collective-permute-done((bf16[768,512]{1,0:T(8,128)(2,1)S(1)}, bf16[768,512]{1,0:T(8,128)(2,1)S(1)}, u32[]{:S(2)}, u32[]{:S(2)}) %collective-permute-start.10) | collective-permute-done | bytes 786464 | tf_op jit(solution)/shard_map/ppermute | solution.py:65
  675.6 12.0 fusion.85
  688.3 17.5 %reduce-scatter.13.cloned.1.call-done = f32[3072,512]{1,0:T(8,128)} async-done(((f32[6144,512]{1,0:T(8,128)}), f32[3072,512]{1,0:T(8,128)}) %reduce-scatter.13.cloned.1.call-update) | async-done | bytes 6291472 | tf_op jit(solution)/shard_map/reduce_scatter | solution.py:72
  716.6 18.7 %all-gather.9.cloned.1.call-done = bf16[6144,512]{1,0:T(8,128)(2,1)} async-done(((bf16[3072,512]{1,0:T(8,128)(2,1)}), bf16[6144,512]{1,0:T(8,128)(2,1)}) %all-gather.9.cloned.1.call-update) | async-done | bytes 6291472 | tf_op jit(solution)/shard_map/all_gather | solution.py:79
  764.8 202.3 %reduce-scatter.19.cloned.1.call-done = f32[768,512]{1,0:T(8,128)} async-done(((f32[6144,512]{1,0:T(8,128)}), f32[768,512]{1,0:T(8,128)}) %reduce-scatter.19.cloned.1.call-update) | async-done | bytes 1572880 | tf_op jit(solution)/shard_map/reduce_scatter | solution.py:88
  972.3 204.9 %reduce-scatter.15.cloned.1.call-done = f32[768,512]{1,0:T(8,128)} async-done(((f32[6144,512]{1,0:T(8,128)}), f32[768,512]{1,0:T(8,128)}) %reduce-scatter.15.cloned.1.call-update) | async-done | bytes 1572880 | tf_op jit(solution)/shard_map/reduce_scatter | solution.py:88
  1182.6 20.4 %collective-permute-done.21 = bf16[768,512]{1,0:T(8,128)(2,1)S(1)} collective-permute-done((bf16[768,512]{1,0:T(8,128)(2,1)S(1)}, bf16[768,512]{1,0:T(8,128)(2,1)S(1)}, u32[]{:S(2)}, u32[]{:S(2)}) %collective-permute-start.21) | collective-permute-done | bytes 786464 | tf_op jit(solution)/shard_map/ppermute | solution.py:65
  1207.8 28.3 %collective-permute-done.22 = bf16[768,512]{1,0:T(8,128)(2,1)S(1)} collective-permute-done((bf16[768,512]{1,0:T(8,128)(2,1)S(1)}, bf16[768,512]{1,0:T(8,128)(2,1)S(1)}, u32[]{:S(2)}, u32[]{:S(2)}) %collective-permute-start.22) | collective-permute-done | bytes 786464 | tf_op jit(solution)/shard_map/ppermute | solution.py:65
  1238.6 16.6 collective-permute-start.26
  1255.1 16.7 collective-permute-done.23
  1274.3 17.1 collective-permute-start.27
  1291.4 15.8 collective-permute-done.24
  1348.5 48.0 %while.27 = (s32[]{:T(128)}, bf16[3,1024,2,64]{1,3,2,0:T(8,128)(2,1)}, bf16[3,1024,2,64]{1,3,2,0:T(8,128)(2,1)}, bf16[3,1024,2,64]{1,3,2,0:T(8,128)(2,1)}, bf16[...) while((s32[]{:T(128)}, ...), condition=%wide.region_25.27_spmd, body=%wide.region_23.26_spmd.sunk | while | flops 1380187136 | bytes 92618056 | solution.py:215
  1403.4 15.9 all-gather.11.cloned.1.call-done
  1472.0 164.9 %reduce-scatter.23.cloned.1.call-done = f32[768,512]{1,0:T(8,128)} async-done(((f32[6144,512]{1,0:T(8,128)}), f32[768,512]{1,0:T(8,128)}) %reduce-scatter.23.cloned.1.call-update) | async-done | bytes 1572880 | tf_op jit(solution)/shard_map/reduce_scatter | solution.py:88
  1639.3 76.0 %all-reduce = (f32[512]{0:T(512)}, f32[512]{0:T(512)}, f32[512]{0:T(512)}, f32[512]{0:T(512)}, f32[512]{0:T(512)}, /*index=5*/f32[512]{0:T(512)}) all-reduce(f32[512]{0:T(512)S(1)} %get-tuple-element.141, f32[512]{0:T(512)S(1)} %get-tuple-element.146, f32[512]{0:T(512)S(1)} %copy-done.37, ...), channel_id=1, replica_groups=mesh['dp'=2,'row'=2,'col'=8] {'dp','col'}, use_global_device_ids=true, to_apply=%region_32.34 | all-reduce | flops 3072 | bytes 24576 | tf_op jit(solution)/shard_map/psum | solution.py:238
  (364 shorter events, 415.8 us)
Async XLA Ops:
  7.2 173.1 %reduce-scatter.9.cloned.1.call-start = ((), (), s32[]{:S(2)}) async-start(), calls=%async_computation.8 | async-start | bytes 14155776 | tf_op jit(solution)/shard_map/reduce_scatter | solution.py:72
  38.2 37.1 %collective-permute-start.4 = (bf16[768,512]{1,0:T(8,128)(2,1)S(1)}, bf16[768,512]{1,0:T(8,128)(2,1)}, u32[]{:S(2)}, u32[]{:S(2)}) collective-permute-start(bf16[768,512]{1,0:T(8,128)(2,1)S(1)} %fusion.75), channel_id=1, source_target_pairs={{0,7},{1,0},{2,1},{3,2},{4,3},{5,4},{6,5},{7,6},{8,15},{9,8},{10,9... | collective-permute-start | bytes 2359304 | tf_op jit(solution)/shard_map/ppermute | solution.py:67
  75.2 36.6 %collective-permute-start.5 = (bf16[768,512]{1,0:T(8,128)(2,1)}, bf16[768,512]{1,0:T(8,128)(2,1)}, u32[]{:S(2)}, u32[]{:S(2)}) collective-permute-start(bf16[768,512]{1,0:T(8,128)(2,1)} %collective-permute-done.4), channel_id=1, source_target_pairs={{0,7},{1,0},{2,1},{3,2},{4,3},{5,4},{6,5},{7,6},{8,15},{9,8},{10,9... | collective-permute-start | bytes 2359304 | tf_op jit(solution)/shard_map/ppermute | solution.py:67
  108.0 35.6 %collective-permute-start.3 = (bf16[768,512]{1,0:T(8,128)(2,1)}, bf16[768,512]{1,0:T(8,128)(2,1)}, u32[]{:S(2)}, u32[]{:S(2)}) collective-permute-start(bf16[768,512]{1,0:T(8,128)(2,1)} %collective-permute-done.2), channel_id=1, source_target_pairs={{0,1},{1,2},{2,3},{3,4},{4,5},{5,6},{6,7},{7,0},{8,9},{9,10},{10,1... | collective-permute-start | bytes 2359304 | tf_op jit(solution)/shard_map/ppermute | solution.py:65
  111.8 38.2 %collective-permute-start.6 = (bf16[768,512]{1,0:T(8,128)(2,1)}, bf16[768,512]{1,0:T(8,128)(2,1)S(1)}, u32[]{:S(2)}, u32[]{:S(2)}) collective-permute-start(bf16[768,512]{1,0:T(8,128)(2,1)} %collective-permute-done.5), channel_id=1, source_target_pairs={{0,7},{1,0},{2,1},{3,2},{4,3},{5,4},{6,5},{7,6},{8,15},{9,8},{10,9... | collective-permute-start | bytes 2359304 | tf_op jit(solution)/shard_map/ppermute | solution.py:67
  164.1 83.2 %all-gather.5.cloned.1.call-start = ((), (), s32[]{:S(2)}) async-start(), calls=%async_computation.9 | async-start | bytes 2359296 | tf_op jit(solution)/shard_map/all_gather | solution.py:79
  236.0 302.7 %reduce-scatter.11.cloned.1.call-start = ((), (), s32[]{:S(2)}) async-start(), calls=%async_computation.10 | async-start | bytes 14155776 | tf_op jit(solution)/shard_map/reduce_scatter | solution.py:88
  255.0 433.2 %reduce-scatter.17.cloned.1.call-start = ((), (), s32[]{:S(2)}) async-start(), calls=%async_computation.14 | async-start | bytes 18874368 | tf_op jit(solution)/shard_map/reduce_scatter | solution.py:72
  289.7 39.1 %collective-permute-start.15 = (bf16[768,512]{1,0:T(8,128)(2,1)S(1)}, bf16[768,512]{1,0:T(8,128)(2,1)S(1)}, u32[]{:S(2)}, u32[]{:S(2)}) collective-permute-start(bf16[768,512]{1,0:T(8,128)(2,1)S(1)} %collective-permute-done.14), channel_id=1, source_target_pairs={{0,1},{1,2},{2,3},{3,4},{4,5},{5,6},{6,7},{7,0},{8,9},{9,10},{10,1... | collective-permute-start | bytes 2359304 | tf_op jit(solution)/shard_map/ppermute | solution.py:65
  290.1 39.1 %collective-permute-start.18 = (bf16[768,512]{1,0:T(8,128)(2,1)S(1)}, bf16[768,512]{1,0:T(8,128)(2,1)S(1)}, u32[]{:S(2)}, u32[]{:S(2)}) collective-permute-start(bf16[768,512]{1,0:T(8,128)(2,1)S(1)} %copy-done.12), channel_id=1, source_target_pairs={{0,7},{1,0},{2,1},{3,2},{4,3},{5,4},{6,5},{7,6},{8,15},{9,8},{10,9... | collective-permute-start | bytes 2359304 | tf_op jit(solution)/shard_map/ppermute | solution.py:67
  328.8 50.1 %collective-permute-start.16 = (bf16[768,512]{1,0:T(8,128)(2,1)S(1)}, bf16[768,512]{1,0:T(8,128)(2,1)S(1)}, u32[]{:S(2)}, u32[]{:S(2)}) collective-permute-start(bf16[768,512]{1,0:T(8,128)(2,1)S(1)} %collective-permute-done.15), channel_id=1, source_target_pairs={{0,1},{1,2},{2,3},{3,4},{4,5},{5,6},{6,7},{7,0},{8,9},{9,10},{10,1... | collective-permute-start | bytes 2359304 | tf_op jit(solution)/shard_map/ppermute | solution.py:65
  329.2 66.7 %collective-permute-start.19 = (bf16[768,512]{1,0:T(8,128)(2,1)S(1)}, bf16[768,512]{1,0:T(8,128)(2,1)S(1)}, u32[]{:S(2)}, u32[]{:S(2)}) collective-permute-start(bf16[768,512]{1,0:T(8,128)(2,1)S(1)} %collective-permute-done.18), channel_id=1, source_target_pairs={{0,7},{1,0},{2,1},{3,2},{4,3},{5,4},{6,5},{7,6},{8,15},{9,8},{10,9... | collective-permute-start | bytes 2359304 | tf_op jit(solution)/shard_map/ppermute | solution.py:67
  378.9 42.1 %collective-permute-start.17 = (bf16[768,512]{1,0:T(8,128)(2,1)S(1)}, bf16[768,512]{1,0:T(8,128)(2,1)S(1)}, u32[]{:S(2)}, u32[]{:S(2)}) collective-permute-start(bf16[768,512]{1,0:T(8,128)(2,1)S(1)} %collective-permute-done.16), channel_id=1, source_target_pairs={{0,1},{1,2},{2,3},{3,4},{4,5},{5,6},{6,7},{7,0},{8,9},{9,10},{10,1... | collective-permute-start | bytes 2359304 | tf_op jit(solution)/shard_map/ppermute | solution.py:65
  395.9 36.9 %collective-permute-start.20 = (bf16[768,512]{1,0:T(8,128)(2,1)S(1)}, bf16[768,512]{1,0:T(8,128)(2,1)S(1)}, u32[]{:S(2)}, u32[]{:S(2)}) collective-permute-start(bf16[768,512]{1,0:T(8,128)(2,1)S(1)} %collective-permute-done.19), channel_id=1, source_target_pairs={{0,7},{1,0},{2,1},{3,2},{4,3},{5,4},{6,5},{7,6},{8,15},{9,8},{10,9... | collective-permute-start | bytes 2359304 | tf_op jit(solution)/shard_map/ppermute | solution.py:67
  447.6 258.2 %reduce-scatter.13.cloned.1.call-start = ((), (), s32[]{:S(2)}) async-start(), calls=%async_computation.11 | async-start | bytes 18874368 | tf_op jit(solution)/shard_map/reduce_scatter | solution.py:72
  565.7 35.9 %collective-permute-start.11 = (bf16[768,512]{1,0:T(8,128)(2,1)S(1)}, bf16[768,512]{1,0:T(8,128)(2,1)S(1)}, u32[]{:S(2)}, u32[]{:S(2)}) collective-permute-start(bf16[768,512]{1,0:T(8,128)(2,1)S(1)} %add_convert_fusion.2), channel_id=1, source_target_pairs={{0,7},{1,0},{2,1},{3,2},{4,3},{5,4},{6,5},{7,6},{8,15},{9,8},{10,9... | collective-permute-start | bytes 2359304 | tf_op jit(solution)/shard_map/ppermute | solution.py:67
  599.1 35.7 %collective-permute-start.9 = (bf16[768,512]{1,0:T(8,128)(2,1)S(1)}, bf16[768,512]{1,0:T(8,128)(2,1)S(1)}, u32[]{:S(2)}, u32[]{:S(2)}) collective-permute-start(bf16[768,512]{1,0:T(8,128)(2,1)S(1)} %collective-permute-done.8), channel_id=1, source_target_pairs={{0,1},{1,2},{2,3},{3,4},{4,5},{5,6},{6,7},{7,0},{8,9},{9,10},{10,1... | collective-permute-start | bytes 2359304 | tf_op jit(solution)/shard_map/ppermute | solution.py:65
  601.6 35.7 %collective-permute-start.12 = (bf16[768,512]{1,0:T(8,128)(2,1)S(1)}, bf16[768,512]{1,0:T(8,128)(2,1)S(1)}, u32[]{:S(2)}, u32[]{:S(2)}) collective-permute-start(bf16[768,512]{1,0:T(8,128)(2,1)S(1)} %collective-permute-done.11), channel_id=1, source_target_pairs={{0,7},{1,0},{2,1},{3,2},{4,3},{5,4},{6,5},{7,6},{8,15},{9,8},{10,9... | collective-permute-start | bytes 2359304 | tf_op jit(solution)/shard_map/ppermute | solution.py:67
  634.9 35.4 %collective-permute-start.10 = (bf16[768,512]{1,0:T(8,128)(2,1)S(1)}, bf16[768,512]{1,0:T(8,128)(2,1)S(1)}, u32[]{:S(2)}, u32[]{:S(2)}) collective-permute-start(bf16[768,512]{1,0:T(8,128)(2,1)S(1)} %collective-permute-done.9), channel_id=1, source_target_pairs={{0,1},{1,2},{2,3},{3,4},{4,5},{5,6},{6,7},{7,0},{8,9},{9,10},{10,1... | collective-permute-start | bytes 2359304 | tf_op jit(solution)/shard_map/ppermute | solution.py:65
  637.3 35.6 %collective-permute-start.13 = (bf16[768,512]{1,0:T(8,128)(2,1)S(1)}, bf16[768,512]{1,0:T(8,128)(2,1)S(1)}, u32[]{:S(2)}, u32[]{:S(2)}) collective-permute-start(bf16[768,512]{1,0:T(8,128)(2,1)S(1)} %collective-permute-done.12), channel_id=1, source_target_pairs={{0,7},{1,0},{2,1},{3,2},{4,3},{5,4},{6,5},{7,6},{8,15},{9,8},{10,9... | collective-permute-start | bytes 2359304 | tf_op jit(solution)/shard_map/ppermute | solution.py:67
  687.6 47.7 %all-gather.9.cloned.1.call-start = ((), (), s32[]{:S(2)}) async-start(), calls=%async_computation.15 | async-start | bytes 9437184 | tf_op jit(solution)/shard_map/all_gather | solution.py:79
  715.8 39.0 %all-gather.7.cloned.1.call-start = ((), (), s32[]{:S(2)}) async-start(), calls=%async_computation.12 | async-start | bytes 9437184 | tf_op jit(solution)/shard_map/all_gather | solution.py:79
  716.6 250.5 %reduce-scatter.19.cloned.1.call-start = ((), (), s32[]{:S(2)}) async-start(), calls=%async_computation.16 | async-start | bytes 14155776 | tf_op jit(solution)/shard_map/reduce_scatter | solution.py:88
  744.9 432.3 %reduce-scatter.15.cloned.1.call-start = ((), (), s32[]{:S(2)}) async-start(), calls=%async_computation.13 | async-start | bytes 14155776 | tf_op jit(solution)/shard_map/reduce_scatter | solution.py:88
  764.1 576.0 %reduce-scatter.21.cloned.1.call-start = ((), (), s32[]{:S(2)}) async-start(), calls=%async_computation.17 | async-start | bytes 4718592 | tf_op jit(solution)/shard_map/reduce_scatter | solution.py:72
  1203.1 35.5 %collective-permute-start.25 = (bf16[768,512]{1,0:T(8,128)(2,1)S(1)}, bf16[768,512]{1,0:T(8,128)(2,1)S(1)}, u32[]{:S(2)}, u32[]{:S(2)}) collective-permute-start(bf16[768,512]{1,0:T(8,128)(2,1)S(1)} %get-tuple-element.214), channel_id=1, source_target_pairs={{0,7},{1,0},{2,1},{3,2},{4,3},{5,4},{6,5},{7,6},{8,15},{9,8},{10,9... | collective-permute-start | bytes 2359304 | tf_op jit(solution)/shard_map/ppermute | solution.py:67
  1236.1 35.7 %collective-permute-start.23 = (bf16[768,512]{1,0:T(8,128)(2,1)S(1)}, bf16[768,512]{1,0:T(8,128)(2,1)S(1)}, u32[]{:S(2)}, u32[]{:S(2)}) collective-permute-start(bf16[768,512]{1,0:T(8,128)(2,1)S(1)} %collective-permute-done.22), channel_id=1, source_target_pairs={{0,1},{1,2},{2,3},{3,4},{4,5},{5,6},{6,7},{7,0},{8,9},{9,10},{10,1... | collective-permute-start | bytes 2359304 | tf_op jit(solution)/shard_map/ppermute | solution.py:65
  1238.6 35.7 %collective-permute-start.26 = (bf16[768,512]{1,0:T(8,128)(2,1)S(1)}, bf16[768,512]{1,0:T(8,128)(2,1)S(1)}, u32[]{:S(2)}, u32[]{:S(2)}) collective-permute-start(bf16[768,512]{1,0:T(8,128)(2,1)S(1)} %collective-permute-done.25), channel_id=1, source_target_pairs={{0,7},{1,0},{2,1},{3,2},{4,3},{5,4},{6,5},{7,6},{8,15},{9,8},{10,9... | collective-permute-start | bytes 2359304 | tf_op jit(solution)/shard_map/ppermute | solution.py:67
  1274.3 39.6 %collective-permute-start.27 = (bf16[768,512]{1,0:T(8,128)(2,1)S(1)}, bf16[768,512]{1,0:T(8,128)(2,1)S(1)}, u32[]{:S(2)}, u32[]{:S(2)}) collective-permute-start(bf16[768,512]{1,0:T(8,128)(2,1)S(1)} %collective-permute-done.26), channel_id=1, source_target_pairs={{0,7},{1,0},{2,1},{3,2},{4,3},{5,4},{6,5},{7,6},{8,15},{9,8},{10,9... | collective-permute-start | bytes 2359304 | tf_op jit(solution)/shard_map/ppermute | solution.py:67
  1329.6 89.6 %all-gather.11.cloned.1.call-start = ((), (), s32[]{:S(2)}) async-start(), calls=%async_computation.18 | async-start | bytes 7077888 | tf_op jit(solution)/shard_map/all_gather | solution.py:79
  1403.3 233.6 %reduce-scatter.23.cloned.1.call-start = ((), (), s32[]{:S(2)}) async-start(), calls=%async_computation.19 | async-start | bytes 14155776 | tf_op jit(solution)/shard_map/reduce_scatter | solution.py:88
  1428.1 297.4 %all-reduce.9.cloned.1.call-start = ((), (), s32[]{:S(2)}) async-start(), calls=%async_computation.20 | async-start | bytes 6291456 | tf_op jit(solution)/shard_map/psum | solution.py:228
  (76 other events, 4298.6 us)
Sparse Core Ops, SparseCore 0:
  164.2 16.0 reduce-scatter.8
  236.1 11.0 all-gather.4
  255.2 283.4 reduce-scatter.10
  540.9 19.8 reduce-scatter.16
  687.8 17.9 reduce-scatter.12
  716.0 19.3 all-gather.8
  736.9 17.9 all-gather.6
  758.4 208.5 reduce-scatter.18
  970.7 206.5 reduce-scatter.14
  1329.7 10.3 reduce-scatter.20
  1403.4 15.7 all-gather.10
  1428.2 208.6 reduce-scatter.22
  1640.5 84.9 all-reduce.8
